TPU v7x, 32 devices: a whole 2x2x4 slice. The times are simulated.
32 devices in a mesh: groups: 2 (over y), tensor: 4 (over z), seq: 2 (over x), section: 2 (over core).
Axes of the slice: x: 2, y: 2, z: 4, core: 2. Of those that a mesh axis runs over, the one named last changes fastest.
Arguments:
- attn_out: bfloat16 [768, 8192], P(('groups', 'seq'), ('tensor', 'section')), parts along dimension 0, may hold values from -6 to 6
- residual: bfloat16 [768, 8192], P(('groups', 'seq'), ('tensor', 'section')), parts along dimension 0, may hold values from -120 to 120
- out_weight: bfloat16 [8192, 8192], P(('tensor', 'section')), may hold values from -0.09375 to 0.09375
- norm_gain: bfloat16 [8192], replicated, may hold values from 0.099609375 to 1.8984375
- gate_up: bfloat16 [8192, 2, 16384], P(None, None, ('tensor', 'seq', 'section')), may hold values from -0.0625 to 0.0625
Outputs:
- stream: bfloat16 [768, 8192], P(('groups', 'seq'), ('tensor', 'section')), parts along dimension 0
- hidden: bfloat16 [768, 16384], P('groups', ('tensor', 'seq', 'section')), parts along dimension 0
There are 2 independent parts, one for each index of `groups`. A program takes and returns all parts, laid end to end along the dimension named above; an argument that names none is the same for every part. Nothing has to cross between parts.
All inputs are finite; a program needn't handle non-finite values.
Results may differ from a plain program's by a relative error of at most 0.012.
Values may be sent and summed in bfloat16 or wider, within the bound.
A program may use at most 192 MiB of HBM per device.

v0:
```python
import jax
import jax.numpy as jnp
from jax import lax
from jax.sharding import PartitionSpec as P

D = 8192


epsilon = 1e-06


def partner(x, axis, distance):
    return lax.ppermute(x, axis, [(i, i ^ 1 << distance) for i in range(lax.axis_size(axis))])


def local(attn_out, residual, out_weight, norm_gain, gate_up):
    axis_size = lax.axis_size(("tensor", "section"))
    position = lax.axis_index(("tensor", "section"))
    row_count, shard_width = attn_out.shape
    partial_value = jnp.dot(attn_out, out_weight, preferred_element_type=jnp.float32).astype(
        jnp.bfloat16
    )
    blocked = partial_value.reshape(row_count, axis_size, shard_width)
    for level_index in range(axis_size.bit_length() - 1):
        paired = blocked.reshape(row_count, blocked.shape[1] // 2, 2, shard_width)
        my_bit = position >> level_index & 1
        kept_half = lax.dynamic_index_in_dim(paired, my_bit, 2, keepdims=False)
        sent_half = lax.dynamic_index_in_dim(paired, 1 - my_bit, 2, keepdims=False)
        received = partner(sent_half, ("tensor", "section"), level_index)
        blocked = (kept_half.astype(jnp.float32) + received.astype(jnp.float32)).astype(
            jnp.bfloat16
        )
    projected = blocked.reshape(row_count, shard_width)
    stream = (projected.astype(jnp.float32) + residual.astype(jnp.float32)).astype(jnp.bfloat16)
    full_stream = lax.all_gather(stream, ("tensor", "section"), axis=1, tiled=True).astype(
        jnp.float32
    )
    totals = jnp.sum(full_stream * full_stream, axis=1, keepdims=True)
    normed_rows = (
        full_stream * lax.rsqrt(totals / D + epsilon) * norm_gain.astype(jnp.float32)
    ).astype(jnp.bfloat16)
    hidden_cols = gate_up.shape[2]
    local_weight = gate_up.reshape(D, 2 * hidden_cols)
    row_block = lax.all_gather(normed_rows, "seq", axis=0, tiled=True)
    products = jnp.dot(row_block, local_weight, preferred_element_type=jnp.float32)
    products = products.reshape(row_block.shape[0], 2, hidden_cols)
    hidden = (jax.nn.silu(products[:, 0]) * products[:, 1]).astype(jnp.bfloat16)
    return (stream, hidden)


def solution(mesh):
    placed = (
        P(("groups", "seq"), ("tensor", "section")),
        P(("groups", "seq"), ("tensor", "section")),
        P(("tensor", "section"), None),
        P(),
        P(None, None, ("tensor", "seq", "section")),
    )
    return jax.shard_map(
        local,
        mesh=mesh,
        in_specs=placed,
        out_specs=(
            P(("groups", "seq"), ("tensor", "section")),
            P("groups", ("tensor", "seq", "section")),
        ),
        check_vma=False,
    )
```

profile of v0, /device:TPU:0, one launch (start us, length us, event | category | flops | bytes accessed | tf_op | source)
XLA Modules:
  0.0 238.3 jit_solution(17975186885308728960)
XLA Ops:
  7.2 0.0 copy-start
  7.2 0.0 all-gather.3.cloned.1.call-start
  7.2 0.9 copy-done
  8.2 10.8 %convolution_convert_fusion = bf16[192,8192]{1,0:T(8,128)(2,1)} fusion(bf16[192,1024]{1,0:T(8,128)(2,1)S(1)} %copy-done, bf16[1024,8192]{1,0:T(8,128)(2,1)} %param.7), kind=kOutput, calls=%fused_computation | convolution fusion | flops 3222798336 | bytes 20316160 | tf_op jit(solution)/shard_map/dot_general | solution.py:20
  19.0 4.9 %reshape_reshape.3 = bf16[192,4,2,1024]{3,2,1,0:T(2,128)(2,1)S(1)} reshape(bf16[192,8192]{1,0:T(8,128)(2,1)} %convolution_convert_fusion) | data formatting | bytes 6291456 | tf_op jit(solution)/shard_map/reshape;reshape | solution.py:25
  23.9 8.4 %constant_dynamic-slice_fusion.2 = (bf16[192,4,1,1024]{3,2,1,0:T(2,128)(2,1)}, bf16[192,4,1,1024]{3,2,1,0:T(2,128)(2,1)S(1)}) fusion(bf16[192,4,2,1024]{3,2,1,0:T(2,128)(2,1)S(1)} %reshape_reshape.3, s32[]{:T(128)S(6)} %select_n.21, s32[]{:T(128)S(6)} %select_n.22), kind=kLoop, calls=%fused_computation.25 | loop fusion | bytes 6291464 | tf_op jit(solution)/shard_map/jit(dynamic_index_in_dim)/dynamic_slice | solution.py:27
  32.3 2.9 %copy.20 = bf16[192,4,1,1024]{3,0,2,1:T(8,128)(2,1)} copy(bf16[192,4,1,1024]{3,2,1,0:T(2,128)(2,1)S(1)} %get-tuple-element.3) | data formatting | bytes 3145728
  35.2 0.5 collective-permute-start
  35.7 3.4 %collective-permute-done = bf16[192,4,1024]{2,0,1:T(8,128)(2,1)} collective-permute-done((bf16[192,4,1024]{2,0,1:T(8,128)(2,1)}, bf16[192,4,1024]{2,0,1:T(8,128)(2,1)}, u32[]{:S(2)}, u32[]{:S(2)}) %collective-permute-start) | collective-permute-done | bytes 1572896 | tf_op jit(solution)/shard_map/ppermute | solution.py:13
  39.0 0.0 copy-done.2
  39.0 3.2 %fusion.5 = bf16[192,4,1024]{2,0,1:T(8,128)(2,1)S(1)} fusion(bf16[192,4,1024]{2,0,1:T(8,128)(2,1)} %collective-permute-done, bf16[192,4,1,1024]{3,2,1,0:T(2,128)(2,1)S(1)} %copy-done.2), kind=kLoop, calls=%fused_computation.9 | loop fusion | flops 3145728 | bytes 4718592 | tf_op jit(solution)/shard_map/convert_element_type | solution.py:30
  42.3 0.0 copy-start.5
  42.3 1.1 copy-done.4
  43.4 0.1 dynamic-slice_bitcast_fusion
  43.5 3.0 %collective-permute-start.1 = (bf16[192,2,1024]{2,0,1:T(8,128)(2,1)S(1)}, bf16[192,2,1024]{2,0,1:T(8,128)(2,1)S(1)}, u32[]{:S(2)}, u32[]{:S(2)}) collective-permute-start(bf16[192,2,1024]{2,0,1:T(8,128)(2,1)S(1)} %dynamic-slice_bitcast_fusion), channel_id=1, source_target_pairs={{0,4},{1,5},{4,0},{5,1},{8,12},{9,13},{12,8},{13,9},{2,6},{3,7},{6... | collective-permute-start | bytes 2359304 | tf_op jit(solution)/shard_map/ppermute | solution.py:13
  46.5 17.8 %collective-permute-done.1 = bf16[192,2,1024]{2,0,1:T(8,128)(2,1)S(1)} collective-permute-done((bf16[192,2,1024]{2,0,1:T(8,128)(2,1)S(1)}, bf16[192,2,1024]{2,0,1:T(8,128)(2,1)S(1)}, u32[]{:S(2)}, u32[]{:S(2)}) %collective-permute-start.1) | collective-permute-done | bytes 786464 | tf_op jit(solution)/shard_map/ppermute | solution.py:13
  64.3 1.4 fusion.8
  65.8 2.8 %collective-permute-start.2 = (bf16[192,1,1024]{2,0,1:T(8,128)(2,1)S(1)}, bf16[192,1,1024]{2,0,1:T(8,128)(2,1)S(1)}, u32[]{:S(2)}, u32[]{:S(2)}) collective-permute-start(bf16[192,1,1024]{2,0,1:T(8,128)(2,1)S(1)} %constant_dynamic-slice_fusion), channel_id=1, source_target_pairs={{0,8},{1,9},{4,12},{5,13},{8,0},{9,1},{12,4},{13,5},{2,10},{3,11},... | collective-permute-start | bytes 1179656 | tf_op jit(solution)/shard_map/ppermute | solution.py:13
  68.6 17.2 %collective-permute-done.2 = bf16[192,1,1024]{2,0,1:T(8,128)(2,1)S(1)} collective-permute-done((bf16[192,1,1024]{2,0,1:T(8,128)(2,1)S(1)}, bf16[192,1,1024]{2,0,1:T(8,128)(2,1)S(1)}, u32[]{:S(2)}, u32[]{:S(2)}) %collective-permute-start.2) | collective-permute-done | bytes 393248 | tf_op jit(solution)/shard_map/ppermute | solution.py:13
  85.8 0.9 fusion.9
  86.7 0.0 all-gather.3.cloned.1.call-update
  86.8 0.3 all-gather.5.cloned.1.call-start
  87.1 39.1 %all-gather.3.cloned.1.call-done = bf16[192,8192]{1,0:T(8,128)(2,1)} async-done(((bf16[192,1024]{1,0:T(8,128)(2,1)}), bf16[192,8192]{1,0:T(8,128)(2,1)}) %all-gather.3.cloned.1.call-update) | async-done | bytes 3145744 | tf_op jit(solution)/shard_map/all_gather | solution.py:35
  126.2 2.8 %fusion = f32[192]{0:T(256)S(1)} fusion(bf16[192,8192]{1,0:T(8,128)(2,1)} %all-gather.3.cloned.1.call-done), kind=kLoop, calls=%fused_computation.3 | loop fusion | flops 4718400 | bytes 3146496 | tf_op jit(solution)/shard_map/reduce_sum | solution.py:38
  128.9 0.1 copy-done.3
  129.0 2.6 %fusion.2 = bf16[192,8192]{1,0:T(8,128)(2,1)} fusion(bf16[192,8192]{1,0:T(8,128)(2,1)S(1)} %copy-done.3, f32[8192]{0:T(1024)S(1)} %convert_element_type.79, f32[192]{0:T(256)S(1)} %add_rsqrt_fusion), kind=kLoop, calls=%fused_computation.5 | loop fusion | flops 6291456 | bytes 6324992 | tf_op jit(solution)/shard_map/convert_element_type | solution.py:41
  131.6 0.0 all-gather.5.cloned.1.call-update
  131.6 24.5 %copy.15 = bf16[1024,8,2,1024]{3,1,2,0:T(8,128)(2,1)} copy(bf16[1024,8,2,1024]{3,2,1,0:T(2,128)(2,1)} %bitcast.43) | data formatting | bytes 67108864
  156.1 40.6 %copy.11 = bf16[2048,8192]{1,0:T(8,128)(2,1)} copy(bf16[2048,8192]{0,1:T(8,128)(2,1)} %bitcast.42) | data formatting | bytes 67108864 | tf_op jit(solution)/shard_map/dot_general | solution.py:45
  196.6 14.4 %all-gather.5.cloned.1.call-done = bf16[384,8192]{1,0:T(8,128)(2,1)} async-done(((bf16[192,8192]{1,0:T(8,128)(2,1)}), bf16[384,8192]{1,0:T(8,128)(2,1)}) %all-gather.5.cloned.1.call-update) | async-done | bytes 6291472 | tf_op jit(solution)/shard_map/all_gather | solution.py:44
  211.0 19.1 %fusion.3 = f32[384,2,1024]{2,0,1:T(8,128)S(1)} fusion(bf16[2,1024,8192]{2,1,0:T(8,128)(2,1)} %bitcast.44, bf16[384,8192]{1,0:T(8,128)(2,1)} %all-gather.5.cloned.1.call-done), kind=kOutput, calls=%fused_computation.6 | convolution fusion | flops 12884901888 | bytes 42991616 | tf_op jit(solution)/shard_map/dot_general | solution.py:45
  230.1 1.4 fusion.7
  (11 shorter events, 0.1 us)
Async XLA Ops:
  7.2 1.0 copy-start
  7.2 119.0 %all-gather.3.cloned.1.call-start = ((), (), s32[]{:S(2)}) async-start(), calls=%async_computation | async-start | bytes 3538944 | tf_op jit(solution)/shard_map/all_gather | solution.py:35
  32.3 6.7 %copy-start.2 = (bf16[192,4,1,1024]{3,2,1,0:T(2,128)(2,1)S(1)}, bf16[192,4,1,1024]{3,2,1,0:T(2,128)(2,1)}, u32[]{:S(2)}) copy-start(bf16[192,4,1,1024]{3,2,1,0:T(2,128)(2,1)} %get-tuple-element.2) | copy-start | bytes 4718596
  35.2 3.9 %collective-permute-start = (bf16[192,4,1024]{2,0,1:T(8,128)(2,1)}, bf16[192,4,1024]{2,0,1:T(8,128)(2,1)}, u32[]{:S(2)}, u32[]{:S(2)}) collective-permute-start(bf16[192,4,1024]{2,0,1:T(8,128)(2,1)} %bitcast.41), channel_id=1, source_target_pairs={{0,1},{1,0},{4,5},{5,4},{8,9},{9,8},{12,13},{13,12},{2,3},{3,2},{6... | collective-permute-start | bytes 4718600 | tf_op jit(solution)/shard_map/ppermute | solution.py:13
  42.3 1.2 copy-start.4
  42.3 43.5 %copy-start.5 = (bf16[192,1024]{1,0:T(8,128)(2,1)S(1)}, bf16[192,1024]{1,0:T(8,128)(2,1)}, u32[]{:S(2)}) copy-start(bf16[192,1024]{1,0:T(8,128)(2,1)} %param.6) | copy-start | bytes 1179652
  43.4 43.6 %copy-start.6 = (bf16[8192]{0:T(1024)(128)(2,1)S(1)}, bf16[8192]{0:T(1024)(128)(2,1)}, u32[]{:S(2)}) copy-start(bf16[8192]{0:T(1024)(128)(2,1)} %param.8) | copy-start | bytes 49156
  43.5 20.8 %collective-permute-start.1 = (bf16[192,2,1024]{2,0,1:T(8,128)(2,1)S(1)}, bf16[192,2,1024]{2,0,1:T(8,128)(2,1)S(1)}, u32[]{:S(2)}, u32[]{:S(2)}) collective-permute-start(bf16[192,2,1024]{2,0,1:T(8,128)(2,1)S(1)} %dynamic-slice_bitcast_fusion), channel_id=1, source_target_pairs={{0,4},{1,5},{4,0},{5,1},{8,12},{9,13},{12,8},{13,9},{2,6},{3,7},{6... | collective-permute-start | bytes 2359304 | tf_op jit(solution)/shard_map/ppermute | solution.py:13
  65.8 20.0 %collective-permute-start.2 = (bf16[192,1,1024]{2,0,1:T(8,128)(2,1)S(1)}, bf16[192,1,1024]{2,0,1:T(8,128)(2,1)S(1)}, u32[]{:S(2)}, u32[]{:S(2)}) collective-permute-start(bf16[192,1,1024]{2,0,1:T(8,128)(2,1)S(1)} %constant_dynamic-slice_fusion), channel_id=1, source_target_pairs={{0,8},{1,9},{4,12},{5,13},{8,0},{9,1},{12,4},{13,5},{2,10},{3,11},... | collective-permute-start | bytes 1179656 | tf_op jit(solution)/shard_map/ppermute | solution.py:13
  86.8 124.2 %all-gather.5.cloned.1.call-start = ((), (), s32[]{:S(2)}) async-start(), calls=%async_computation.1 | async-start | bytes 9437184 | tf_op jit(solution)/shard_map/all_gather | solution.py:44
  126.2 2.8 %copy-start.3 = (bf16[192,8192]{1,0:T(8,128)(2,1)S(1)}, bf16[192,8192]{1,0:T(8,128)(2,1)}, u32[]{:S(2)}) copy-start(bf16[192,8192]{1,0:T(8,128)(2,1)} %all-gather.3.cloned.1.call-done) | copy-start | bytes 9437188
  211.0 20.5 %copy-start.1 = (bf16[192,1024]{1,0:T(8,128)(2,1)S(1)}, bf16[192,1024]{1,0:T(8,128)(2,1)}, u32[]{:S(2)}) copy-start(bf16[192,1024]{1,0:T(8,128)(2,1)} %param.5) | copy-start | bytes 1179652
Sparse Core Ops, SparseCore 0:
  86.9 39.2 all-gather.2
  131.7 79.2 all-gather.4
where the time goes:
time: 240 us; the launch traced here: 238 us
  waiting for transfers between devices  91.9 us (38%)
  local copies, waits for them, and re-layouts  83.5 us (35%)
  matrix products  29.9 us (12%)
  between operations  14.1 us (6%)
  other arithmetic  12.3 us (5%)
  starting transfers between devices  6.61 us (3%)
    dot_general x1, local copies, waits for them, and re-layouts, local(): jnp.dot(row_block, local_weight, preferred_element_type=jnp.float32)  40.6 us
    all_gather x1, waiting for transfers between devices, local(): lax.all_gather(stream, ('tensor', 'section'), axis=1, tiled=True)  39.1 us
    ppermute x3, waiting for transfers between devices, partner(): lax.ppermute(x, axis, [(i, i ^ 1 << distance) for i in range(lax.axis_siz...  38.4 us
    unnamed x16, local copies, waits for them, and re-layouts  29.5 us
    dot_general x1, matrix products, local(): jnp.dot(row_block, local_weight, preferred_element_type=jnp.float32)  19.1 us
    all_gather x1, waiting for transfers between devices, local(): row_block = lax.all_gather(normed_rows, 'seq', axis=0, tiled=True)  14.4 us
    dot_general x1, matrix products, local(): jnp.dot(attn_out, out_weight, preferred_element_type=jnp.float32)  10.8 us
    dynamic_slice x1, local copies, waits for them, and re-layouts, local(): kept_half = lax.dynamic_index_in_dim(paired, my_bit, 2, keepdims=False)  8.36 us
  transfers between devices with their start and end apart: 5, of which 5 were waited for; matrix products, arithmetic and copies ran while one was open for 27% of the time, Pallas kernels for 0%

commit v1 on v0

--- a/solution.py
+++ b/solution.py
@@ -1,6 +1,8 @@
 import jax
 import jax.numpy as jnp
 from jax import lax
+from jax.experimental import pallas as pl
+from jax.experimental.pallas import tpu as pltpu
 from jax.sharding import PartitionSpec as P
 
 D = 8192
@@ -48,6 +50,389 @@
     return (stream, hidden)
 
 
+CHUNKS = 4
+RAW_SLOTS = 4
+ORDER = (1, 3, 0, 2)
+
+
+def fused_kernel(
+    attn_ref,
+    residual_ref,
+    gain_ref,
+    weight_hbm,
+    gate_up_hbm,
+    stream_ref,
+    hidden_ref,
+    weight_ring,
+    raw_ring,
+    weights,
+    sent_part,
+    kept_part,
+    got0,
+    got1,
+    got2,
+    blocks,
+    scaled,
+    acc,
+    squares,
+    weight_sem,
+    raw_sem,
+    send0,
+    recv0,
+    send1,
+    recv1,
+    send2,
+    recv2,
+    send_right,
+    send_left,
+    send_seq,
+    send_own,
+    send_other,
+    recv_block,
+):
+    t = lax.axis_index("tensor")
+    q = lax.axis_index("seq")
+    s = lax.axis_index("section")
+    nt = lax.axis_size("tensor")
+    rows, width = attn_ref.shape
+    sub = width // CHUNKS
+    n_block = 2 * nt
+    hidden_cols = hidden_ref.shape[1]
+    depth = weights.shape[1]
+    f32, bf16 = jnp.float32, jnp.bfloat16
+
+    def relative(r):
+        return ((t // 2 + r // 2) % 2) * 2 + (t + r % 2) % 2
+
+    def remote(src, dst, ssem, rsem, **where):
+        return pltpu.make_async_remote_copy(
+            src_ref=src,
+            dst_ref=dst,
+            send_sem=ssem,
+            recv_sem=rsem,
+            device_id=where,
+            device_id_type=pl.DeviceIdType.MESH,
+        )
+
+    def weight_copy(c, j, half):
+        section = (1 - s) if half == 0 else s
+        column = (relative(ORDER[j]) * 2 + section) * width + c * sub
+        return pltpu.make_async_copy(
+            weight_hbm.at[:, pl.ds(pl.multiple_of(column, sub), sub)],
+            weight_ring.at[2 * j + half],
+            weight_sem.at[2 * j + half],
+        )
+
+    def raw_copy(k):
+        start = (k % n_block) * width + (k // n_block) * sub
+        slot = k % RAW_SLOTS
+        return pltpu.make_async_copy(
+            gate_up_hbm.at[pl.ds(pl.multiple_of(start, sub), sub)],
+            raw_ring.at[slot],
+            raw_sem.at[slot],
+        )
+
+    def copy0(c, r):
+        return remote(
+            sent_part.at[c, r], got0.at[c, r], send0.at[c, r], recv0.at[c, r], section=1 - s
+        )
+
+    def copy1(c, h):
+        return remote(
+            kept_part.at[c, 2 * h + 1],
+            got1.at[c, h],
+            send1.at[c, h],
+            recv1.at[c, h],
+            tensor=relative(1),
+        )
+
+    def copy2(c):
+        return remote(
+            kept_part.at[c, 2], got2.at[c], send2.at[c], recv2.at[c], tensor=relative(2)
+        )
+
+    def copy_block(qq, c, o, sems, **where):
+        b = o * 2 + s
+        here = blocks.at[qq, c, b]
+        return remote(here, here, sems.at[c, o], recv_block.at[qq, c, b], **where)
+
+    def await_block(qq, c, b):
+        here = blocks.at[qq, c, b]
+        remote(
+            here, here, send_own.at[c, 0], recv_block.at[qq, c, b], section=1 - s
+        ).wait_recv()
+
+    for j in range(4):
+        for half in range(2):
+            weight_copy(0, j, half).start()
+    barrier = pltpu.get_barrier_semaphore()
+    for d in range(1, nt):
+        pl.semaphore_signal(barrier, inc=1, device_id={"tensor": (t + d) % nt}, device_id_type=pl.DeviceIdType.MESH)
+    pl.semaphore_signal(barrier, inc=1, device_id={"seq": 1 - q}, device_id_type=pl.DeviceIdType.MESH)
+    pl.semaphore_signal(barrier, inc=1, device_id={"section": 1 - s}, device_id_type=pl.DeviceIdType.MESH)
+    for k in range(RAW_SLOTS):
+        raw_copy(k).start()
+    pl.semaphore_wait(barrier, nt + 1)
+
+    def project(c):
+        for j, r in enumerate(ORDER):
+            for half in range(2):
+                weight_copy(c, j, half).wait()
+                part = jnp.dot(
+                    attn_ref[...], weight_ring[2 * j + half], preferred_element_type=f32
+                ).astype(bf16)
+                (sent_part, kept_part)[half][c, r] = part
+
+                @pl.when(c + 1 < CHUNKS)
+                def _():
+                    weight_copy(c + 1, j, half).start()
+
+                if half == 0:
+                    copy0(c, r).start()
+
+    def add_section(c):
+        for r in ORDER:
+            copy0(c, r).wait_recv()
+            kept_part[c, r] = (
+                kept_part[c, r].astype(f32) + got0[c, r].astype(f32)
+            ).astype(bf16)
+            if r % 2:
+                copy1(c, r // 2).start()
+
+    def unpack(c):
+        @pl.loop(0, n_block)
+        def _(b):
+            k = c * n_block + b
+            raw_copy(k).wait()
+            both = pltpu.einshape("kgn->gkn", raw_ring[k % RAW_SLOTS])
+            place = pl.ds(pl.multiple_of(b * sub, sub), sub)
+            weights[c, place, :hidden_cols] = both[0]
+            weights[c, place, hidden_cols:] = both[1]
+
+            @pl.when(k + RAW_SLOTS < CHUNKS * n_block)
+            def _():
+                raw_copy(k + RAW_SLOTS).start()
+
+    def add_near(c):
+        for h in (1, 0):
+            copy1(c, h).wait_recv()
+            kept_part[c, 2 * h] = (
+                kept_part[c, 2 * h].astype(f32) + got1[c, h].astype(f32)
+            ).astype(bf16)
+            if h:
+                copy2(c).start()
+
+    def finish_stream(c):
+        copy2(c).wait_recv()
+        projected = (kept_part[c, 0].astype(f32) + got2[c].astype(f32)).astype(bf16)
+        columns = pl.ds(pl.multiple_of(c * sub, sub), sub)
+        stream = (projected.astype(f32) + residual_ref[:, columns].astype(f32)).astype(bf16)
+        blocks[q, c, t * 2 + s] = stream
+        stream_ref[:, columns] = stream
+
+        @pl.when(t < nt - 1)
+        def _():
+            copy_block(q, c, t, send_right, tensor=t + 1).start()
+
+        @pl.when(t > 0)
+        def _():
+            copy_block(q, c, t, send_left, tensor=t - 1).start()
+
+        copy_block(q, c, t, send_seq, seq=1 - q).start()
+        copy_block(q, c, t, send_own, section=1 - s).start()
+
+    def forward(c, d):
+        @pl.when(t >= d)
+        def _():
+            o = t - d
+            await_block(q, c, o * 2 + s)
+
+            @pl.when(t < nt - 1)
+            def _():
+                copy_block(q, c, o, send_right, tensor=t + 1).start()
+
+            copy_block(q, c, o, send_seq, seq=1 - q).start()
+            copy_block(q, c, o, send_own, section=1 - s).start()
+
+        @pl.when(t + d < nt)
+        def _():
+            o = t + d
+            await_block(q, c, o * 2 + s)
+
+            @pl.when(t > 0)
+            def _():
+                copy_block(q, c, o, send_left, tensor=t - 1).start()
+
+            copy_block(q, c, o, send_seq, seq=1 - q).start()
+            copy_block(q, c, o, send_own, section=1 - s).start()
+
+    def hand_over(c, d):
+        def one(o):
+            await_block(1 - q, c, o * 2 + s)
+            copy_block(1 - q, c, o, send_other, section=1 - s).start()
+
+        if d == 0:
+            one(t)
+        else:
+
+            @pl.when(t >= d)
+            def _():
+                one(t - d)
+
+            @pl.when(t + d < nt)
+            def _():
+                one(t + d)
+
+    def multiply(qq, c):
+        for o in range(nt):
+            await_block(qq, c, o * 2 + 1 - s)
+
+        @pl.loop(0, n_block)
+        def _(b):
+            x = blocks[qq, c, b].astype(f32)
+            gain = gain_ref[:, pl.ds(pl.multiple_of(b * width + c * sub, sub), sub)].astype(f32)
+            scaled[:, pl.ds(pl.multiple_of(b * sub, sub), sub)] = (x * gain).astype(bf16)
+            square = x * x
+            total = square[:, :128]
+            for k in range(1, sub // 128):
+                total = total + square[:, k * 128 : (k + 1) * 128]
+            squares[qq] += total
+
+        tile = 512
+
+        @pl.loop(0, 2 * hidden_cols // tile)
+        def _(n):
+            columns = pl.ds(pl.multiple_of(n * tile, tile), tile)
+            acc[qq, :, columns] += jnp.dot(
+                scaled[...], weights[c, :, columns], preferred_element_type=f32
+            )
+
+    acc[...] = jnp.zeros_like(acc)
+    squares[...] = jnp.zeros_like(squares)
+    stages = (
+        (0, project),
+        (0, add_section),
+        (1, add_near),
+        (2, finish_stream),
+        (3, lambda c: forward(c, 1)),
+        (4, lambda c: forward(c, 2)),
+        (5, lambda c: forward(c, 3)),
+        (3, lambda c: hand_over(c, 0)),
+        (4, lambda c: hand_over(c, 1)),
+        (5, lambda c: hand_over(c, 2)),
+        (6, lambda c: hand_over(c, 3)),
+        (0, unpack),
+        (6, lambda c: multiply(q, c)),
+        (7, lambda c: multiply(1 - q, c)),
+    )
+
+    @pl.loop(0, CHUNKS + 7)
+    def _(step):
+        for lag, stage in stages:
+
+            @pl.when(jnp.logical_and(step >= lag, step < lag + CHUNKS))
+            def _():
+                stage(step - lag)
+
+    for qq in range(2):
+        mean_square = jnp.sum(squares[qq], axis=1, keepdims=True) / (n_block * width)
+        scale = lax.rsqrt(mean_square + epsilon)
+        tile = 256
+
+        @pl.loop(0, hidden_cols // tile)
+        def _(n):
+            gate = acc[qq, :, pl.ds(pl.multiple_of(n * tile, tile), tile)] * scale
+            up = acc[qq, :, pl.ds(pl.multiple_of(hidden_cols + n * tile, tile), tile)] * scale
+            hidden_ref[qq * rows : (qq + 1) * rows, pl.ds(pl.multiple_of(n * tile, tile), tile)] = (
+                gate / (1.0 + jnp.exp(-gate)) * up
+            ).astype(bf16)
+
+    @pl.loop(0, CHUNKS)
+    def _(c):
+        for r in range(4):
+            copy0(c, r).wait_send()
+        for h in range(2):
+            copy1(c, h).wait_send()
+        copy2(c).wait_send()
+        for o in range(nt):
+            copy_block(q, c, o, send_seq, seq=1 - q).wait_send()
+            copy_block(q, c, o, send_own, section=1 - s).wait_send()
+            copy_block(1 - q, c, o, send_other, section=1 - s).wait_send()
+
+            @pl.when(jnp.logical_and(o <= t, t < nt - 1))
+            def _():
+                copy_block(q, c, o, send_right, tensor=(t + 1) % nt).wait_send()
+
+            @pl.when(jnp.logical_and(o >= t, t > 0))
+            def _():
+                copy_block(q, c, o, send_left, tensor=(t + nt - 1) % nt).wait_send()
+
+
+def fused(attn_out, residual, out_weight, norm_gain, gate_up):
+    rows, width = attn_out.shape
+    nt = lax.axis_size("tensor")
+    hidden_cols = gate_up.shape[2]
+    sub = width // CHUNKS
+    depth = gate_up.shape[0] // CHUNKS
+    vmem = pl.BlockSpec(memory_space=pltpu.VMEM)
+    hbm = pl.BlockSpec(memory_space=pl.ANY)
+    dma = pltpu.SemaphoreType.DMA
+    bf16, f32 = jnp.bfloat16, jnp.float32
+    return pl.pallas_call(
+        fused_kernel,
+        name="layer_window",
+        out_shape=(
+            jax.ShapeDtypeStruct((rows, width), bf16),
+            jax.ShapeDtypeStruct((2 * rows, hidden_cols), bf16),
+        ),
+        in_specs=[vmem, vmem, vmem, hbm, hbm],
+        out_specs=(vmem, vmem),
+        scratch_shapes=[
+            pltpu.VMEM((8, width, sub), bf16),
+            pltpu.VMEM((RAW_SLOTS, sub, 2, hidden_cols), bf16),
+            pltpu.VMEM((CHUNKS, depth, 2 * hidden_cols), bf16),
+            pltpu.VMEM((CHUNKS, 4, rows, sub), bf16),
+            pltpu.VMEM((CHUNKS, 4, rows, sub), bf16),
+            pltpu.VMEM((CHUNKS, 4, rows, sub), bf16),
+            pltpu.VMEM((CHUNKS, 2, rows, sub), bf16),
+            pltpu.VMEM((CHUNKS, rows, sub), bf16),
+            pltpu.VMEM((2, CHUNKS, 2 * nt, rows, sub), bf16),
+            pltpu.VMEM((rows, depth), bf16),
+            pltpu.VMEM((2, rows, 2 * hidden_cols), f32),
+            pltpu.VMEM((2, rows, 128), f32),
+            dma((8,)),
+            dma((RAW_SLOTS,)),
+            dma((CHUNKS, 4)),
+            dma((CHUNKS, 4)),
+            dma((CHUNKS, 2)),
+            dma((CHUNKS, 2)),
+            dma((CHUNKS,)),
+            dma((CHUNKS,)),
+            dma((CHUNKS, nt)),
+            dma((CHUNKS, nt)),
+            dma((CHUNKS, nt)),
+            dma((CHUNKS, nt)),
+            dma((CHUNKS, nt)),
+            dma((2, CHUNKS, 2 * nt)),
+        ],
+        compiler_params=pltpu.CompilerParams(
+            collective_id=0, has_side_effects=True, vmem_limit_bytes=66 * 1024 * 1024 - 2 * 1024 * 1024 - 65536
+        ),
+    )(attn_out, residual, norm_gain.reshape(1, -1), out_weight, gate_up)
+
+
+def fits_fused(mesh, attn_out, gate_up):
+    rows, width = attn_out.shape
+    return (
+        (mesh.shape["tensor"], mesh.shape["seq"], mesh.shape["section"]) == (4, 2, 2)
+        and rows % 16 == 0
+        and width % (128 * CHUNKS) == 0
+        and gate_up.shape[2] % 256 == 0
+        and 2 * gate_up.size <= 34 * 1024 * 1024
+        and rows * width <= 192 * 1024
+    )
+
+
 def solution(mesh):
     placed = (
         P(("groups", "seq"), ("tensor", "section")),
@@ -56,8 +441,11 @@
         P(),
         P(None, None, ("tensor", "seq", "section")),
     )
+    def step(*args):
+        return (fused if fits_fused(mesh, args[0], args[4]) else local)(*args)
+
     return jax.shard_map(
-        local,
+        step,
         mesh=mesh,
         in_specs=placed,
         out_specs=(

time: 240 us -> 93.3 us (0.39)
  waiting for transfers between devices: 91.9 us -> 0 us
  Pallas kernels: 0 us -> 87.2 us
  local copies, waits for them, and re-layouts: 83.5 us -> 5.18 us
  matrix products: 29.9 us -> 0 us
  between operations: 14.1 us -> 0.64 us
  other arithmetic: 12.3 us -> 0 us
  starting transfers between devices: 6.61 us -> 0 us
    pallas_call x0 -> x1, Pallas kernels: none -> 87.2 us  [fused(): pl.pallas_call(fused_kernel, name='layer_window', out_shape=(jax.ShapeDty...]
    all_gather x2 -> x0, waiting for transfers between devices: 53.4 us -> none  [the longest x1 39.1 us: local(): lax.all_gather(stream, ('tensor', 'section'), axis=1, tiled=True)]
    dot_general x1 -> x0, local copies, waits for them, and re-layouts: 40.6 us -> none  [local(): jnp.dot(row_block, local_weight, preferred_element_type=jnp.float32)]
    ppermute x3 -> x0, waiting for transfers between devices: 38.4 us -> none  [partner(): lax.ppermute(x, axis, [(i, i ^ 1 << distance) for i in range(lax.axis_siz...]
    dot_general x2 -> x0, matrix products: 29.9 us -> none  [the longest x1 19.1 us: local(): jnp.dot(row_block, local_weight, preferred_element_type=jnp.float32)]
    unnamed x16 -> x2, local copies, waits for them, and re-layouts: 29.5 us -> 3.83 us
    convert_element_type x6 -> x0, other arithmetic: 9.53 us -> none  [the longest x2 4.66 us: local(): (kept_half.astype(jnp.float32) + received.astype(jnp.float32)).astype(jnp...]
    dynamic_slice x1 -> x0, local copies, waits for them, and re-layouts: 8.36 us -> none  [local(): kept_half = lax.dynamic_index_in_dim(paired, my_bit, 2, keepdims=False)]
  transfers between devices with their start and end apart: 5 -> 0, of which waited for: 5 -> 0; matrix products, arithmetic and copies ran while one was open for 27% -> 0% of each run, Pallas kernels for 0% -> 0%
where the time goes in v1:
time: 93.3 us; the launch traced here: 93 us
  Pallas kernels  87.2 us (93%)
  local copies, waits for them, and re-layouts  5.18 us (6%)
    pallas_call x1, Pallas kernels, fused(): pl.pallas_call(fused_kernel, name='layer_window', out_shape=(jax.ShapeDty...  87.2 us
    unnamed x2, local copies, waits for them, and re-layouts  3.83 us

profile of v1, /device:TPU:0, one launch (start us, length us, event | category | flops | bytes accessed | tf_op | source)
XLA Modules:
  0.0 93.0 jit_solution(5422479884270481877)
XLA Ops:
  0.6 1.4 %reshape.7.gain_ref = bf16[1,8192]{1,0:T(2,128)(2,1)} reshape(bf16[8192]{0:T(1024)(128)(2,1)} %param.8) | data formatting | bytes 32768 | tf_op jit(solution)/shard_map/reshape | solution.py:421
  2.0 87.2 %layer_window.1 = (bf16[192,1024]{1,0:T(8,128)(2,1)}, bf16[384,1024]{1,0:T(8,128)(2,1)}) custom-call(bf16[192,1024]{1,0:T(8,128)(2,1)} %attn_ref.1, bf16[192,1024]{1,0:T(8,128)(2,1)} %residual_ref.1, bf16[1,8192]{1,0:T(2,128)(2,1)} %reshape.7.gain_ref, bf16[1024,8192]{1,0:T(8,128)(2,1)} %weight_hbm.1, bf16[8192,2,1024]{2,1,0:T(2,128)(2,1)} %gate_up_hbm.1), custom_call_target="tpu_custom_call" | custom-call | tf_op jit(solution)/shard_map/layer_window/pallas_call | solution.py:381
  89.2 1.8 %copy.9 = bf16[192,1024]{1,0:T(8,128)(2,1)} copy(bf16[192,1024]{1,0:T(8,128)(2,1)} %get-tuple-element.4) | data formatting | bytes 786432
  91.0 2.1 %copy.10 = bf16[384,1024]{1,0:T(8,128)(2,1)} copy(bf16[384,1024]{1,0:T(8,128)(2,1)} %get-tuple-element.5) | data formatting | bytes 1572864

commit v2 on v1

--- a/solution.py
+++ b/solution.py
@@ -310,6 +310,9 @@
     acc[...] = jnp.zeros_like(acc)
     squares[...] = jnp.zeros_like(squares)
     stages = (
+        (3, unpack),
+        (6, lambda c: multiply(q, c)),
+        (7, lambda c: multiply(1 - q, c)),
         (0, project),
         (0, add_section),
         (1, add_near),
@@ -321,9 +324,6 @@
         (4, lambda c: hand_over(c, 1)),
         (5, lambda c: hand_over(c, 2)),
         (6, lambda c: hand_over(c, 3)),
-        (0, unpack),
-        (6, lambda c: multiply(q, c)),
-        (7, lambda c: multiply(1 - q, c)),
     )
 
     @pl.loop(0, CHUNKS + 7)

time: 93.3 us -> 88.2 us (0.945)
  Pallas kernels: 87.2 us -> 82.1 us
    pallas_call x1, Pallas kernels: 87.2 us -> 82.1 us  [fused(): pl.pallas_call(fused_kernel, name='layer_window', out_shape=(jax.ShapeDty...]
where the time goes in v2:
time: 88.2 us; the launch traced here: 87.9 us
  Pallas kernels  82.1 us (93%)
  local copies, waits for them, and re-layouts  5.18 us (6%)
    pallas_call x1, Pallas kernels, fused(): pl.pallas_call(fused_kernel, name='layer_window', out_shape=(jax.ShapeDty...  82.1 us
    unnamed x2, local copies, waits for them, and re-layouts  3.83 us

profile of v2, /device:TPU:0, one launch (start us, length us, event | category | flops | bytes accessed | tf_op | source)
XLA Modules:
  0.0 87.9 jit_solution(14108288578842544110)
XLA Ops:
  0.6 1.4 %reshape.7.gain_ref = bf16[1,8192]{1,0:T(2,128)(2,1)} reshape(bf16[8192]{0:T(1024)(128)(2,1)} %param.8) | data formatting | bytes 32768 | tf_op jit(solution)/shard_map/reshape | solution.py:421
  2.0 82.1 %layer_window.1 = (bf16[192,1024]{1,0:T(8,128)(2,1)}, bf16[384,1024]{1,0:T(8,128)(2,1)}) custom-call(bf16[192,1024]{1,0:T(8,128)(2,1)} %attn_ref.1, bf16[192,1024]{1,0:T(8,128)(2,1)} %residual_ref.1, bf16[1,8192]{1,0:T(2,128)(2,1)} %reshape.7.gain_ref, bf16[1024,8192]{1,0:T(8,128)(2,1)} %weight_hbm.1, bf16[8192,2,1024]{2,1,0:T(2,128)(2,1)} %gate_up_hbm.1), custom_call_target="tpu_custom_call" | custom-call | tf_op jit(solution)/shard_map/layer_window/pallas_call | solution.py:381
  84.1 1.8 %copy.9 = bf16[192,1024]{1,0:T(8,128)(2,1)} copy(bf16[192,1024]{1,0:T(8,128)(2,1)} %get-tuple-element.4) | data formatting | bytes 786432
  85.8 2.1 %copy.10 = bf16[384,1024]{1,0:T(8,128)(2,1)} copy(bf16[384,1024]{1,0:T(8,128)(2,1)} %get-tuple-element.5) | data formatting | bytes 1572864
